TPU v7x, 128 devices: a whole 4x4x4 slice. The times are simulated.
128 devices in a mesh: req: 16 (over z, x_hi, core), head: 8 (over y, x_lo).
Axes of the slice: x: 4 (x_hi: 2, x_lo: 2; x = x_hi * 2 + x_lo), y: 4, z: 4, core: 2. Of those that a mesh axis runs over, the one named last changes fastest.
Arguments:
- hidden_in: bfloat16 [128, 8192], P('head', 'req'), may hold values from -40 to 40
- attn_gain: bfloat16 [8192], P('req'), may hold values from 0.5 to 1.5
- w_qkv: bfloat16 [8192, 10240], P('req', 'head'), may hold values from -0.0625 to 0.0625
- w_out: bfloat16 [8192, 8192], P('head', 'req'), may hold values from -0.0625 to 0.0625
- k_cache: bfloat16 [128, 4096, 1024], P('req', None, 'head'), may hold values from -400 to 400
- v_cache: bfloat16 [128, 4096, 1024], P('req', None, 'head'), may hold values from -6 to 6
- lengths: int32 [128], P('req'), may hold values from 1 to 4096, 135168 in all
Outputs:
- hidden_out: bfloat16 [128, 8192], P('head', 'req')
Inputs may be any that keep to these rules, and one draw needn't show every extreme that they name: One request holds exactly 4096 tokens; the lengths add up to 135168.
All inputs are finite; a program needn't handle non-finite values. No bound on the sum of `lengths` on one device may be relied on, other than what follows from the above.
Results may differ from a plain program's by a relative error of at most 0.0055.
Values may be sent and summed in bfloat16 or wider, within the bound.
A program may use at most 64 MiB of HBM per device.

v0:
```python
import jax
import jax.numpy as jnp
from jax import lax
from jax.sharding import PartitionSpec as P

D = 8192
GROUP = 8
HD = 128
epsilon = 1e-05
rope_base = 500000.0


def rotate(vectors, positions):
    halfway = vectors.shape[-1] // 2
    frequency = jnp.exp(
        -jnp.log(rope_base) * 2.0 * jnp.arange(halfway, dtype=jnp.float32) / vectors.shape[-1]
    )
    angles = positions.astype(jnp.float32)[:, None] * frequency[None, :]
    target_shape = (angles.shape[0],) + (1,) * (vectors.ndim - 2) + (halfway,)
    cosine = jnp.cos(angles).reshape(target_shape)
    sine_part = jnp.sin(angles).reshape(target_shape)
    first = vectors[..., :halfway]
    second = vectors[..., halfway:]
    return jnp.concatenate(
        [first * cosine - second * sine_part, second * cosine + first * sine_part], axis=-1
    )


def own_part(own_score, running, totals, new_values):
    own_prob = lax.optimization_barrier(
        (jnp.exp(own_score - running) / totals).astype(jnp.bfloat16)
    )
    return own_prob.astype(jnp.float32)[..., None] * new_values.astype(jnp.float32)[:, :, None, :]


def attend_padded(queries, new_keys, new_values, cached_keys, cached_values, lengths, factor):
    slots = cached_keys.shape[1]
    inside = jnp.arange(slots, dtype=jnp.int32)[None, :] < lengths[:, None]
    scores = (
        jnp.einsum("rkgd,rpkd->rkgp", queries, cached_keys, preferred_element_type=jnp.float32)
        * factor
    )
    scores = jnp.where(inside[:, None, None, :], scores, -1e30)
    own_score = (
        jnp.einsum("rkgd,rkd->rkg", queries, new_keys, preferred_element_type=jnp.float32) * factor
    )
    running = jnp.maximum(jnp.max(scores, axis=3), own_score)
    weights = jnp.where(inside[:, None, None, :], jnp.exp(scores - running[..., None]), 0.0)
    totals = jnp.sum(weights, axis=3) + jnp.exp(own_score - running)
    probs = (weights / totals[..., None]).astype(jnp.bfloat16)
    mixed = jnp.einsum("rkgp,rpkd->rkgd", probs, cached_values, preferred_element_type=jnp.float32)
    mixed = mixed + own_part(own_score, running, totals, new_values)
    return mixed.astype(jnp.bfloat16)


def local(hidden_in, attn_gain, w_qkv, w_out, k_cache, v_cache, lengths):
    states = hidden_in.astype(jnp.float32)
    every_row = lax.all_gather(hidden_in, "head", axis=0, tiled=True).astype(jnp.float32)
    scaled = (every_row * attn_gain.astype(jnp.float32)[None, :]).astype(jnp.bfloat16)
    partial_square = jnp.sum(every_row * every_row, axis=1)
    partial = jnp.dot(scaled, w_qkv, preferred_element_type=jnp.float32)
    columns = partial.shape[1]
    packed = jnp.concatenate(
        [partial, jnp.broadcast_to(partial_square[:, None], (partial.shape[0], 128))], axis=1
    )
    summed = lax.psum_scatter(packed, "req", scatter_dimension=0, tiled=True)
    mean_square = summed[:, columns] / D
    own_count = k_cache.shape[0]
    slots = k_cache.shape[1]
    local_heads = k_cache.shape[2] // HD
    projected = summed[:, :columns] * lax.rsqrt(mean_square + epsilon)[:, None]
    projected = projected.reshape(own_count, local_heads, GROUP + 2, HD)
    queries = rotate(projected[:, :, :GROUP], lengths).astype(jnp.bfloat16)
    new_keys = rotate(projected[:, :, GROUP], lengths).astype(jnp.bfloat16)
    new_values = projected[:, :, GROUP + 1].astype(jnp.bfloat16)
    cached_keys = k_cache.reshape(own_count, slots, local_heads, HD)
    cached_values = v_cache.reshape(own_count, slots, local_heads, HD)
    factor = HD ** (-0.5)
    attended = attend_padded(
        queries, new_keys, new_values, cached_keys, cached_values, lengths, factor
    )
    flat_rows = attended.reshape(own_count, local_heads * GROUP * HD)
    gathered = lax.all_gather(flat_rows, "req", axis=0, tiled=True)
    output = lax.psum_scatter(
        jnp.dot(gathered, w_out, preferred_element_type=jnp.float32),
        "head",
        scatter_dimension=0,
        tiled=True,
    )
    return (states + output).astype(jnp.bfloat16)


def solution(mesh):
    return jax.shard_map(
        local,
        mesh=mesh,
        in_specs=(
            P("head", "req"),
            P("req"),
            P("req", "head"),
            P("head", "req"),
            P("req", None, "head"),
            P("req", None, "head"),
            P("req"),
        ),
        out_specs=P("head", "req"),
        check_vma=False,
    )
```

profile of v0, /device:TPU:0, one launch (start us, length us, event | category | flops | bytes accessed | tf_op | source)
XLA Modules:
  0.0 255.5 jit_solution(280369030877171777)
XLA Ops:
  6.5 29.1 %all_gather.6 = bf16[128,512]{1,0:T(8,128)(2,1)S(1)} all-gather(bf16[16,512]{1,0:T(8,128)(2,1)} %param.7), channel_id=1, replica_groups=mesh['req'=16,'head'=8] {'head'}, dimensions={0}, use_global_device_ids=true | all-gather | bytes 147456 | tf_op jit(solution)/shard_map/all_gather | solution.py:58
  35.6 0.7 convert_element_type.53
  36.3 0.1 fusion.9
  36.4 0.3 fusion.10
  36.7 0.1 broadcast_in_dim.21
  36.8 0.9 pad_maximum_fusion
  37.8 0.7 convert_element_type.55
  38.5 1.2 dynamic-slice
  40.4 0.1 multiply_cosine_fusion.1
  40.5 0.7 iota_compare_fusion
  41.2 137.7 %all-reduce.3.cloned.1.call-done = f32[128,1408]{1,0:T(8,128)} async-done(((f32[128,1408]{1,0:T(8,128)}), f32[128,1408]{1,0:T(8,128)}) %all-reduce.3.cloned.1.call-update) | async-done | bytes 720912
  178.9 1.0 fusion.26
  179.9 1.1 fusion.13
  181.0 0.1 fusion.38
  181.1 0.1 fusion.33
  181.2 0.1 maximum_bitcast_fusion
  181.3 0.2 fusion.27
  181.5 5.8 %fusion.39 = (f32[8,8]{1,0:T(8,128)S(1)}, f32[8,8,4096]{2,1,0:T(8,128)S(1)}) fusion(bf16[8,4096,128]{2,1,0:T(8,128)(2,1)} %param.11, bf16[8,8,64]{2,1,0:T(8,128)(2,1)S(1)} %get-tuple-element.6, bf16[8,8,64]{2,1,0:T(8,128)(2,1)S(1)} %get-tuple-element.5, pred[8,4096]{1,0:T(8,128)(4,1)S(1)} %iota_compare_fusion), kind=kOutput, calls=%fused_computation.65 | convolution fusion | flops 67928000 | bytes 9486592 | tf_op jit(solution)/shard_map/rkgd,rpkd->rkgp/dot_general | solution.py:40
  187.3 0.4 fusion.3
  187.8 1.3 fusion.2
  189.1 20.8 %all_gather.7 = bf16[128,1024]{1,0:T(8,128)(2,1)S(1)} all-gather(bf16[8,1024]{1,0:T(8,128)(2,1)S(1)} %bitcast.37), channel_id=1, replica_groups=mesh['req'=16,'head'=8] {'req'}, dimensions={0}, use_global_device_ids=true | all-gather | bytes 278528 | tf_op jit(solution)/shard_map/all_gather | solution.py:83
  209.9 1.0 fusion.40
  210.9 36.3 %reduce-scatter.2.cloned.1.call-done = f32[16,512]{1,0:T(8,128)} async-done(((f32[128,512]{1,0:T(8,128)}), f32[16,512]{1,0:T(8,128)}) %reduce-scatter.2.cloned.1.call-update) | async-done | bytes 32784 | tf_op jit(solution)/shard_map/reduce_scatter | solution.py:84
  247.3 1.4 add_convert_fusion
  (20 shorter events, 0.2 us)
Async XLA Ops:
  6.5 29.9 %copy-start = (bf16[512,1280]{1,0:T(8,128)(2,1)S(1)}, bf16[512,1280]{1,0:T(8,128)(2,1)}, u32[]{:S(2)}) copy-start(bf16[512,1280]{1,0:T(8,128)(2,1)} %param.9) | copy-start | bytes 3932164
  6.5 172.4 %all-reduce.3.cloned.1.call-start = ((), (), s32[]{:S(2)}) async-start(), calls=%async_computation.2 | async-start | bytes 1441792
  37.8 209.5 %reduce-scatter.2.cloned.1.call-start = ((), (), s32[]{:S(2)}) async-start(), calls=%async_computation.1 | async-start | bytes 294912 | tf_op jit(solution)/shard_map/reduce_scatter | solution.py:84
  178.9 8.8 %copy-start.1 = (bf16[8,4096,128]{2,1,0:T(8,128)(2,1)S(1)}, bf16[8,4096,128]{2,1,0:T(8,128)(2,1)}, u32[]{:S(2)}) copy-start(bf16[8,4096,128]{2,1,0:T(8,128)(2,1)} %param.12) | copy-start | bytes 25165828
  187.7 22.2 %copy-start.2 = (bf16[1024,512]{1,0:T(8,128)(2,1)S(1)}, bf16[1024,512]{1,0:T(8,128)(2,1)}, u32[]{:S(2)}) copy-start(bf16[1024,512]{1,0:T(8,128)(2,1)} %param.10) | copy-start | bytes 3145732
  187.7 59.5 %copy-start.3 = (bf16[16,512]{1,0:T(8,128)(2,1)S(1)}, bf16[16,512]{1,0:T(8,128)(2,1)}, u32[]{:S(2)}) copy-start(bf16[16,512]{1,0:T(8,128)(2,1)} %param.7) | copy-start | bytes 49156
Sparse Core Ops, SparseCore 0:
  37.9 140.9 all-reduce.2
  211.1 36.1 reduce-scatter.1
where the time goes:
time: 256 us; the launch traced here: 255 us
  waiting for transfers between devices  174 us (68%)
  blocking collectives  49.8 us (19%)
  between operations  14.1 us (6%)
  matrix products  8.67 us (3%)
  other arithmetic  7.34 us (3%)
    unnamed x3, waiting for transfers between devices  138 us
    reduce_scatter x1, waiting for transfers between devices, local(): lax.psum_scatter(jnp.dot(gathered, w_out, preferred_element_type=jnp.floa...  36.3 us
    all_gather x1, blocking collectives, local(): lax.all_gather(hidden_in, 'head', axis=0, tiled=True).astype(jnp.float32)  29.1 us
    all_gather x1, blocking collectives, local(): gathered = lax.all_gather(flat_rows, 'req', axis=0, tiled=True)  20.8 us
    dot_general x1, matrix products, attend_padded(): jnp.einsum('rkgd,rpkd->rkgp', queries, cached_keys, preferred_element_typ...  5.77 us
  transfers between devices with their start and end apart: 2, of which 2 were waited for; matrix products, arithmetic and copies ran while one was open for 1% of the time, Pallas kernels for 0%

commit v1 on v0

--- a/solution.py
+++ b/solution.py
@@ -8,6 +8,18 @@
 HD = 128
 epsilon = 1e-05
 rope_base = 500000.0
+
+
+def trails_cover(inputs):
+    return jnp.concatenate(
+        lax.all_to_all(
+            jnp.stack(lax.axis_size("head") * [inputs], 0),
+            concat_axis=0,
+            split_axis=0,
+            axis_name="head",
+        ),
+        0,
+    )
 
 
 def rotate(vectors, positions):
@@ -55,7 +67,7 @@
 
 def local(hidden_in, attn_gain, w_qkv, w_out, k_cache, v_cache, lengths):
     states = hidden_in.astype(jnp.float32)
-    every_row = lax.all_gather(hidden_in, "head", axis=0, tiled=True).astype(jnp.float32)
+    every_row = trails_cover(hidden_in).astype(jnp.float32)
     scaled = (every_row * attn_gain.astype(jnp.float32)[None, :]).astype(jnp.bfloat16)
     partial_square = jnp.sum(every_row * every_row, axis=1)
     partial = jnp.dot(scaled, w_qkv, preferred_element_type=jnp.float32)

time: 256 us -> 238 us (0.930)
  blocking collectives: 49.8 us -> 20.8 us
  starting transfers between devices: 0.04 us -> 5.56 us
  waiting for transfers between devices: 174 us -> 178 us
    all_gather x1 -> x0, blocking collectives: 29.1 us -> none  [local(): lax.all_gather(hidden_in, 'head', axis=0, tiled=True).astype(jnp.float32)]
    all_to_all x0 -> x1, starting transfers between devices: none -> 5.48 us  [trails_cover(): lax.all_to_all(jnp.stack(lax.axis_size('head') * [inputs], 0), concat_axi...]
    all_to_all x0 -> x1, waiting for transfers between devices: none -> 3.29 us  [trails_cover(): lax.all_to_all(jnp.stack(lax.axis_size('head') * [inputs], 0), concat_axi...]
  transfers between devices with their start and end apart: 2 -> 3, of which waited for: 2 -> 3; matrix products, arithmetic and copies ran while one was open for 1% -> 1% of each run, Pallas kernels for 0% -> 0%
where the time goes in v1:
time: 238 us
  waiting for transfers between devices  178 us (75%)
  blocking collectives  20.8 us (9%)
  between operations  14.2 us (6%)
  matrix products  8.67 us (4%)
  other arithmetic  7.34 us (3%)
  starting transfers between devices  5.56 us (2%)
  local copies, waits for them, and re-layouts  2.98 us (1%)
    unnamed x3, waiting for transfers between devices  139 us
    reduce_scatter x1, waiting for transfers between devices, local(): lax.psum_scatter(jnp.dot(gathered, w_out, preferred_element_type=jnp.floa...  36.3 us
    all_gather x1, blocking collectives, local(): gathered = lax.all_gather(flat_rows, 'req', axis=0, tiled=True)  20.8 us
    dot_general x1, matrix products, attend_padded(): jnp.einsum('rkgd,rpkd->rkgp', queries, cached_keys, preferred_element_typ...  5.77 us
    all_to_all x1, starting transfers between devices, trails_cover(): lax.all_to_all(jnp.stack(lax.axis_size('head') * [inputs], 0), concat_axi...  5.48 us
  transfers between devices with their start and end apart: 3, of which 3 were waited for; matrix products, arithmetic and copies ran while one was open for 1% of the time, Pallas kernels for 0%

profile of v1, /device:TPU:0, one launch (start us, length us, event | category | flops | bytes accessed | tf_op | source)
XLA Modules:
  0.0 237.7 jit_solution(4649466943314515733)
XLA Ops:
  6.5 1.5 stack.2
  8.0 5.5 %all-to-all-start = ((bf16[8,16,512]{2,1,0:T(8,128)(2,1)}), bf16[8,16,512]{2,1,0:T(8,128)(2,1)S(1)}, u32[]{:S(2)}, u32[]{:S(2)}) async-start(bf16[8,16,512]{2,1,0:T(8,128)(2,1)} %stack.2), calls=%async_computation | async-start | bytes 262144 | tf_op jit(solution)/shard_map/all_to_all | solution.py:15
  13.6 0.7 convert_element_type.60
  14.2 0.7 convert_element_type.63
  14.9 1.2 dynamic-slice
  16.8 0.1 multiply_cosine_fusion.1
  16.9 3.3 %all-to-all-done = bf16[8,16,512]{2,1,0:T(8,128)(2,1)S(1)} async-done(((bf16[8,16,512]{2,1,0:T(8,128)(2,1)}), bf16[8,16,512]{2,1,0:T(8,128)(2,1)S(1)}, u32[]{:S(2)}, u32[]{:S(2)}) %all-to-all-start) | async-done | bytes 131104 | tf_op jit(solution)/shard_map/all_to_all | solution.py:15
  20.2 0.1 multiply_reduce_fusion
  20.3 0.1 broadcast_in_dim.23
  20.4 0.3 fusion.36
  20.9 0.9 pad_maximum_fusion
  21.9 0.7 iota_compare_fusion
  22.6 138.6 %all-reduce.3.cloned.1.call-done = f32[128,1408]{1,0:T(8,128)} async-done(((f32[128,1408]{1,0:T(8,128)}), f32[128,1408]{1,0:T(8,128)}) %all-reduce.3.cloned.1.call-update) | async-done | bytes 720912
  161.2 1.0 fusion.22
  162.2 1.1 fusion.9
  163.3 0.1 fusion.29
  163.6 0.2 fusion.23
  163.8 5.8 %fusion.35 = (f32[8,8]{1,0:T(8,128)S(1)}, f32[8,8,4096]{2,1,0:T(8,128)S(1)}) fusion(bf16[8,4096,128]{2,1,0:T(8,128)(2,1)} %param.11, bf16[8,8,64]{2,1,0:T(8,128)(2,1)S(1)} %get-tuple-element.6, bf16[8,8,64]{2,1,0:T(8,128)(2,1)S(1)} %get-tuple-element.5, pred[8,4096]{1,0:T(8,128)(4,1)S(1)} %iota_compare_fusion), kind=kOutput, calls=%fused_computation.62 | convolution fusion | flops 67928000 | bytes 9486592 | tf_op jit(solution)/shard_map/rkgd,rpkd->rkgp/dot_general | solution.py:52
  169.5 0.4 fusion.3
  170.0 1.3 fusion.2
  171.4 20.8 %all_gather.3 = bf16[128,1024]{1,0:T(8,128)(2,1)S(1)} all-gather(bf16[8,1024]{1,0:T(8,128)(2,1)S(1)} %bitcast.42), channel_id=1, replica_groups=mesh['req'=16,'head'=8] {'req'}, dimensions={0}, use_global_device_ids=true | all-gather | bytes 278528 | tf_op jit(solution)/shard_map/all_gather | solution.py:95
  192.2 1.0 fusion.37
  193.2 36.3 %reduce-scatter.2.cloned.1.call-done = f32[16,512]{1,0:T(8,128)} async-done(((f32[128,512]{1,0:T(8,128)}), f32[16,512]{1,0:T(8,128)}) %reduce-scatter.2.cloned.1.call-update) | async-done | bytes 32784 | tf_op jit(solution)/shard_map/reduce_scatter | solution.py:96
  229.5 1.4 add_convert_fusion
  (24 shorter events, 0.5 us)
Async XLA Ops:
  6.5 13.9 %copy-start = (bf16[512,1280]{1,0:T(8,128)(2,1)S(1)}, bf16[512,1280]{1,0:T(8,128)(2,1)}, u32[]{:S(2)}) copy-start(bf16[512,1280]{1,0:T(8,128)(2,1)} %param.9) | copy-start | bytes 3932164
  8.0 12.2 %all-to-all-start = ((bf16[8,16,512]{2,1,0:T(8,128)(2,1)}), bf16[8,16,512]{2,1,0:T(8,128)(2,1)S(1)}, u32[]{:S(2)}, u32[]{:S(2)}) async-start(bf16[8,16,512]{2,1,0:T(8,128)(2,1)} %stack.2), calls=%async_computation | async-start | bytes 262144 | tf_op jit(solution)/shard_map/all_to_all | solution.py:15
  13.5 147.7 %all-reduce.3.cloned.1.call-start = ((), (), s32[]{:S(2)}) async-start(), calls=%async_computation.3 | async-start | bytes 1441792
  21.8 207.7 %reduce-scatter.2.cloned.1.call-start = ((), (), s32[]{:S(2)}) async-start(), calls=%async_computation.2 | async-start | bytes 294912 | tf_op jit(solution)/shard_map/reduce_scatter | solution.py:96
  161.2 8.8 %copy-start.1 = (bf16[8,4096,128]{2,1,0:T(8,128)(2,1)S(1)}, bf16[8,4096,128]{2,1,0:T(8,128)(2,1)}, u32[]{:S(2)}) copy-start(bf16[8,4096,128]{2,1,0:T(8,128)(2,1)} %param.12) | copy-start | bytes 25165828
  170.0 22.2 %copy-start.2 = (bf16[1024,512]{1,0:T(8,128)(2,1)S(1)}, bf16[1024,512]{1,0:T(8,128)(2,1)}, u32[]{:S(2)}) copy-start(bf16[1024,512]{1,0:T(8,128)(2,1)} %param.10) | copy-start | bytes 3145732
  170.0 59.5 %copy-start.3 = (bf16[16,512]{1,0:T(8,128)(2,1)S(1)}, bf16[16,512]{1,0:T(8,128)(2,1)}, u32[]{:S(2)}) copy-start(bf16[16,512]{1,0:T(8,128)(2,1)} %param.7) | copy-start | bytes 49156
Sparse Core Ops, SparseCore 0:
  21.9 139.2 all-reduce.2
  193.3 36.1 reduce-scatter.1
